TPU v7x, 512 devices: a whole 4x4x16 slice. The times are simulated.
512 devices in a mesh: dp: 32 (over y_hi, z), expert: 16 (over y_lo, x, core).
Axes of the slice: x: 4, y: 4 (y_hi: 2, y_lo: 2; y = y_hi * 2 + y_lo), z: 16, core: 2. Of those that a mesh axis runs over, the one named last changes fastest.
Arguments:
- residual_in: bfloat16 [1536, 2048], P('dp', 'expert'), may hold values from -36 to 36
- attention_values: bfloat16 [1536, 2048], P('dp', 'expert'), may hold values from -6 to 6
- out_weight: bfloat16 [2048, 2048], P('expert', 'dp'), may hold values from -0.25 to 0.25
- norm_gain: float32 [2048], replicated, may hold values from 0.1 to 1.9
- shared_gate: bfloat16 [2816, 2048], P('expert'), may hold values from -0.125 to 0.125
- shared_up: bfloat16 [2816, 2048], P('expert'), may hold values from -0.125 to 0.125
- shared_down: bfloat16 [2816, 2048], P('expert'), may hold values from -0.15625 to 0.15625
- expert_gate: bfloat16 [64, 1408, 2048], P('dp', 'expert'), may hold values from -0.125 to 0.125
- expert_up: bfloat16 [64, 1408, 2048], P('dp', 'expert'), may hold values from -0.125 to 0.125
- expert_down: bfloat16 [64, 1408, 2048], P('dp', 'expert'), may hold values from -0.21875 to 0.21875
- expert_ids: int32 [1536, 6], P('dp'), may hold values from 0 to 63, all different within a row; in each aligned block of 48 rows (0 to 47, 48 to 95, ...) at most 10 rows name the same one
- gate_weights: float32 [1536, 6], P('dp'), may hold values from 0.02 to 0.5
Outputs:
- layer_out: bfloat16 [1536, 2048], P('dp', 'expert')
Inputs may be any that keep to these rules, and one draw needn't show every extreme that they name: `expert_ids`: each token names 6 different experts; among the 48 tokens of one index of dp (aligned blocks of rows) no expert is named by more than 10 tokens, a bound that some block reaches.
All inputs are finite; a program needn't handle non-finite values.
Results may differ from a plain program's by a relative error of at most 0.0035.
Values may be sent and summed in bfloat16 or wider, within the bound.
A program may use at most 128 MiB of HBM per device.

v0:
```python
import jax
import jax.numpy as jnp
from jax import lax
from jax.sharding import PartitionSpec as P

epsilon = 1e-06


def by_rows(left, right):
    return lax.dot_general(
        left, right, (((1,), (1,)), ((), ())), preferred_element_type=jnp.float32
    )


def expert_slots(expert_ids, experts, capacity):
    token_count, choose = expert_ids.shape
    flat_ids = expert_ids.reshape(-1)
    matches = (flat_ids[:, None] == jnp.arange(experts, dtype=jnp.int32)[None, :]).astype(jnp.int32)
    earlier = jnp.cumsum(matches, axis=0) - matches
    target = flat_ids * capacity + jnp.sum(earlier * matches, axis=1)
    return target.reshape(token_count, choose)


def collect_rows(returned_rows, slot_index, gate_weights):
    token_count, choose = slot_index.shape
    picked = returned_rows[slot_index.reshape(-1)].reshape(
        token_count, choose, returned_rows.shape[1]
    )
    return jnp.sum(picked * gate_weights[:, :, None], axis=1)


def expert_apply(buffer, expert_gate, expert_up, expert_down):
    gate_part = jnp.einsum(
        "slmd,lfd->slmf", buffer, expert_gate, preferred_element_type=jnp.float32
    )
    up_part = jnp.einsum("slmd,lfd->slmf", buffer, expert_up, preferred_element_type=jnp.float32)
    active = (jax.nn.silu(gate_part) * up_part).astype(jnp.bfloat16)
    return jnp.einsum("slmf,lfd->slmd", active, expert_down, preferred_element_type=jnp.float32)


def shards(
    residual_in,
    attention_values,
    out_weight,
    norm_gain,
    shared_gate,
    shared_up,
    shared_down,
    expert_gate,
    expert_up,
    expert_down,
    expert_ids,
    gate_weights,
):
    row_count = residual_in.shape[0]
    slice_width = residual_in.shape[1]
    expert_size = lax.axis_size("expert")
    batch_size = lax.axis_size("dp")
    full_width = slice_width * expert_size
    local_experts = expert_gate.shape[0]
    experts = local_experts * batch_size
    choose = expert_ids.shape[1]
    capacity = 2 * ((row_count * choose + experts - 1) // experts)
    column_start = lax.axis_index("expert") * slice_width
    head_terms = jnp.dot(
        attention_values,
        lax.all_gather(out_weight, "dp", axis=1, tiled=True),
        preferred_element_type=jnp.float32,
    )
    residual_own = residual_in.astype(jnp.float32)
    current = lax.dynamic_slice_in_dim(head_terms, column_start, slice_width, 1)
    head_terms = lax.dynamic_update_slice_in_dim(
        head_terms, current + residual_own, column_start, 1
    )
    residual = lax.psum(head_terms, "expert")
    inverse_rms = lax.rsqrt(jnp.mean(residual * residual, axis=1, keepdims=True) + epsilon)
    normed = (residual * inverse_rms * norm_gain).astype(jnp.bfloat16)
    residual_slice = lax.dynamic_slice_in_dim(residual, column_start, slice_width, 1)
    shared_active = (jax.nn.silu(by_rows(normed, shared_gate)) * by_rows(normed, shared_up)).astype(
        jnp.bfloat16
    )
    shared_terms = jnp.dot(shared_active, shared_down, preferred_element_type=jnp.float32)
    slot_index = expert_slots(expert_ids, experts, capacity)
    places = (
        slot_index[:, :, None] == jnp.arange(experts * capacity, dtype=jnp.int32)[None, None, :]
    )
    selector = jnp.any(places, axis=1).astype(jnp.bfloat16)
    slot_rows = lax.dot_general(
        selector, normed, (((0,), (0,)), ((), ())), preferred_element_type=jnp.float32
    )
    buffer = slot_rows.astype(jnp.bfloat16).reshape(batch_size, local_experts, capacity, full_width)
    partials = expert_apply(
        lax.all_to_all(buffer, "dp", split_axis=0, concat_axis=0, tiled=True),
        expert_gate,
        expert_up,
        expert_down,
    )
    returned = lax.all_to_all(partials, "dp", split_axis=0, concat_axis=0, tiled=True)
    routed_terms = collect_rows(
        returned.reshape(experts * capacity, full_width), slot_index, gate_weights
    )
    totals = lax.psum_scatter(
        shared_terms + routed_terms, "expert", scatter_dimension=1, tiled=True
    )
    return (residual_slice + totals).astype(jnp.bfloat16)


def solution(mesh):
    return jax.shard_map(
        shards,
        mesh=mesh,
        in_specs=(
            P("dp", "expert"),
            P("dp", "expert"),
            P("expert", "dp"),
            P(),
            P("expert", None),
            P("expert", None),
            P("expert", None),
            P("dp", "expert", None),
            P("dp", "expert", None),
            P("dp", "expert", None),
            P("dp", None),
            P("dp", None),
        ),
        out_specs=P("dp", "expert"),
        check_vma=False,
    )
```

profile of v0, /device:TPU:1, one launch (start us, length us, event | category | flops | bytes accessed | tf_op | source)
XLA Modules:
  0.0 722.6 jit_solution(14739102939381321039)
XLA Ops:
  6.5 0.0 copy-start
  6.5 0.0 copy-start.6
  6.5 0.0 all-reduce.3.cloned.1.call-start
  6.5 72.7 %all_gather.3 = bf16[128,2048]{0,1:T(8,128)(2,1)S(1)} all-gather(bf16[128,64]{0,1:T(8,128)(2,1)} %param.14), channel_id=1, replica_groups=mesh['dp'=32,'expert'=16] {'dp'}, dimensions={1}, use_global_device_ids=true | all-gather | bytes 540672 | tf_op jit(solution)/shard_map/all_gather | solution.py:67
  79.3 1.0 fusion.42
  80.2 0.7 add_dynamic-update-slice_fusion
  81.0 0.0 copy-start.1
  81.0 0.7 copy-done.1
  81.7 0.0 all-reduce.3.cloned.1.call-update
  81.7 0.8 copy.41
  82.5 0.1 eq.35
  82.7 0.9 reduce-window.6
  83.6 0.2 slice_reduce_fusion
  83.8 0.1 bitcast_bitcast_fusion
  84.0 0.1 reduce_sum.33
  84.1 0.6 broadcast_multiply_fusion
  84.7 0.1 copy.45
  84.8 0.8 fusion.19
  85.6 131.6 %all-reduce.3.cloned.1.call-done = f32[48,2048]{1,0:T(8,128)} async-done(((f32[48,2048]{1,0:T(8,128)}), f32[48,2048]{1,0:T(8,128)}) %all-reduce.3.cloned.1.call-update) | async-done | bytes 393232 | tf_op jit(solution)/shard_map/psum | solution.py:75
  217.2 1.1 multiply_reduce_fusion.1
  218.3 0.0 copy-done.6
  218.3 1.1 multiply_convert_fusion
  219.4 1.6 convolution_convert_fusion
  221.1 2.8 reshape.68
  223.9 4.9 copy.46
  228.8 0.0 copy-start.8
  228.8 135.8 %all_to_all.10 = bf16[32,2,10,2048]{3,1,2,0:T(2,128)(2,1)S(1)} all-to-all(bf16[32,2,10,2048]{3,1,2,0:T(2,128)(2,1)S(1)} %copy.46), channel_id=1, replica_groups=mesh['dp'=32,'expert'=16] {'dp'}, dimensions={0} | all-to-all | bytes 5242880 | tf_op jit(solution)/shard_map/all_to_all | solution.py:93
  364.6 0.0 copy-done.8
  364.6 2.3 fusion.4
  366.9 0.0 copy-done
  366.9 5.9 convolution_bitcast_fusion
  372.8 8.8 %copy.49 = f32[32,2,10,2048]{3,1,2,0:T(2,128)} copy(f32[32,2,10,2048]{3,0,2,1:T(8,128)} %convolution_bitcast_fusion) | data formatting | bytes 10485760 | tf_op jit(solution)/shard_map/slmf,lfd->slmd/transpose | solution.py:38
  381.6 0.0 copy-start.5
  381.6 0.0 copy-start.7
  381.6 0.0 copy-start.4
  381.6 6.4 all-to-all-start.1
  388.0 0.3 reduce-scatter.2.cloned.1.call-start
  388.3 0.0 copy-done.5
  388.3 0.1 mul.78
  388.4 0.0 copy-done.7
  388.4 0.1 copy.51
  388.6 0.0 copy-done.4
  388.6 0.3 fusion.43
  388.9 229.6 %all-to-all-done.1 = f32[32,2,10,2048]{3,1,2,0:T(2,128)} async-done(((f32[32,2,10,2048]{3,1,2,0:T(2,128)}), f32[32,2,10,2048]{3,1,2,0:T(2,128)}, u32[]{:S(2)}, u32[]{:S(2)}) %all-to-all-start.1) | async-done | bytes 5242912 | tf_op jit(solution)/shard_map/all_to_all | solution.py:98
  618.6 10.3 %copy.50 = f32[32,2,10,2048]{3,2,1,0:T(8,128)} copy(f32[32,2,10,2048]{3,1,2,0:T(2,128)} %all-to-all-done.1) | data formatting | bytes 10485760 | tf_op jit(solution)/shard_map/all_to_all | solution.py:98
  628.9 7.4 %reshape.69 = f32[640,2048]{1,0:T(8,128)} reshape(f32[32,2,10,2048]{3,2,1,0:T(8,128)} %copy.50) | data formatting | bytes 10485760 | tf_op jit(solution)/shard_map/reshape | solution.py:100
  636.3 6.8 gather_fusion
  643.1 1.8 reshape.70
  644.9 0.0 copy-start.2
  644.9 0.0 copy-start.3
  644.9 3.1 multiply_reduce_fusion
  648.0 0.0 copy-done.2
  648.1 0.0 copy-done.3
  648.1 1.4 convolution_add_fusion
  649.5 0.0 reduce-scatter.2.cloned.1.call-update
  649.5 64.9 %reduce-scatter.2.cloned.1.call-done = f32[48,128]{1,0:T(8,128)} async-done(((f32[48,2048]{1,0:T(8,128)}), f32[48,128]{1,0:T(8,128)}) %reduce-scatter.2.cloned.1.call-update) | async-done | bytes 24592 | tf_op jit(solution)/shard_map/reduce_scatter | solution.py:102
  714.4 1.4 add_convert_fusion
  (7 shorter events, 0.1 us)
Async XLA Ops:
  6.5 360.3 %copy-start = (bf16[2,88,2048]{2,1,0:T(8,128)(2,1)S(1)}, bf16[2,88,2048]{2,1,0:T(8,128)(2,1)}, u32[]{:S(2)}) copy-start(bf16[2,88,2048]{2,1,0:T(8,128)(2,1)} %param.21) | copy-start | bytes 2162692
  6.5 211.8 %copy-start.6 = (f32[2048]{0:T(1024)S(1)}, f32[2048]{0:T(1024)}, u32[]{:S(2)}) copy-start(f32[2048]{0:T(1024)} %param.15) | copy-start | bytes 24580
  6.5 210.6 %all-reduce.3.cloned.1.call-start = ((), (), s32[]{:S(2)}) async-start(), calls=%async_computation.3 | async-start | bytes 786432 | tf_op jit(solution)/shard_map/psum | solution.py:75
  81.0 0.7 copy-start.1
  228.8 135.8 %copy-start.8 = (bf16[2,88,2048]{2,1,0:T(8,128)(2,1)S(1)}, bf16[2,88,2048]{2,1,0:T(8,128)(2,1)}, u32[]{:S(2)}) copy-start(bf16[2,88,2048]{2,1,0:T(8,128)(2,1)} %param.19) | copy-start | bytes 2162692
  381.6 6.7 copy-start.5
  381.6 6.8 copy-start.7
  381.6 7.0 copy-start.4
  381.6 237.0 %all-to-all-start.1 = ((f32[32,2,10,2048]{3,1,2,0:T(2,128)}), f32[32,2,10,2048]{3,1,2,0:T(2,128)}, u32[]{:S(2)}, u32[]{:S(2)}) async-start(f32[32,2,10,2048]{3,1,2,0:T(2,128)} %copy.49), calls=%async_computation.1 | async-start | bytes 10485760 | tf_op jit(solution)/shard_map/all_to_all | solution.py:98
  388.0 326.4 %reduce-scatter.2.cloned.1.call-start = ((), (), s32[]{:S(2)}) async-start(), calls=%async_computation.4 | async-start | bytes 417792 | tf_op jit(solution)/shard_map/reduce_scatter | solution.py:102
  644.9 3.1 copy-start.2
  644.9 3.2 copy-start.3
Sparse Core Ops, SparseCore 0:
  81.9 135.2 all-reduce.2
  649.6 64.7 reduce-scatter.1
where the time goes:
time: 725 us; the launch traced here: 723 us
  waiting for transfers between devices  426 us (59%)
  blocking collectives  208 us (29%)
  local copies, waits for them, and re-layouts  45.1 us (6%)
  between operations  13.6 us (2%)
  matrix products  12.6 us (2%)
  other arithmetic  9.98 us (1%)
    all_to_all x1, waiting for transfers between devices, shards(): lax.all_to_all(partials, 'dp', split_axis=0, concat_axis=0, tiled=True)  230 us
    all_to_all x1, blocking collectives, shards(): lax.all_to_all(buffer, 'dp', split_axis=0, concat_axis=0, tiled=True)  136 us
    psum x1, waiting for transfers between devices, shards(): residual = lax.psum(head_terms, 'expert')  132 us
    all_gather x1, blocking collectives, shards(): lax.all_gather(out_weight, 'dp', axis=1, tiled=True)  72.7 us
    reduce_scatter x1, waiting for transfers between devices, shards(): lax.psum_scatter(shared_terms + routed_terms, 'expert', scatter_dimension...  64.9 us
  transfers between devices with their start and end apart: 3, of which 3 were waited for; matrix products, arithmetic and copies ran while one was open for 1% of the time, Pallas kernels for 0%

commit v1 on v0

v1 whole, which is shorter than its diff:
```python
import jax
import jax.numpy as jnp
from jax import lax
from jax.experimental import pallas as pl
from jax.experimental.pallas import tpu as pltpu
from jax.sharding import PartitionSpec as P

MESH = pl.DeviceIdType.MESH
epsilon = 1e-06
DP = 32
EX = 16
CAP = 10
RB = 32
LANE = 128
F32 = jnp.float32
BF16 = jnp.bfloat16


def by_rows(left, right):
    return lax.dot_general(left, right, (((1,), (1,)), ((), ())), preferred_element_type=F32)


def by_columns(left, right):
    return lax.dot_general(left, right, (((0,), (0,)), ((), ())), preferred_element_type=F32)


def iota(shape, dim):
    return lax.broadcasted_iota(jnp.int32, shape, dim)


def silu(v):
    return v / (1.0 + jnp.exp(-v))


def loop(start, stop, body):
    def step(j, carry):
        body(j)
        return carry

    lax.fori_loop(start, stop, step, 0)


def layer_kernel(
    res_in, attn, w_in, gain, sh_gate, sh_up, sh_down, ex_gate, ex_up, ex_down, ids, weights,
    out,
    wt, w_all, part, rs_buf, res_all, normed, xs, xr, x_all, a_all, d_all, s_part, s_buf, ys, yr,
    pack, unpack, sel, comb,
    w_send, w_recv, d_send, d_recv, r_send, r_recv, g_send, g_recv, x_send, x_recv,
    xa_send, xa_recv, s_send, s_recv, aa_send, aa_recv, y_send, y_recv, own_sem,
):
    d = lax.axis_index("dp")
    e = lax.axis_index("expert")
    rows = res_in.shape[0]
    hidden = ex_gate.shape[1]
    locals_ = ex_gate.shape[0]
    per_expert = DP * CAP

    def rcopy(src, dst, send, recv, device):
        return pltpu.make_async_remote_copy(
            src_ref=src, dst_ref=dst, send_sem=send, recv_sem=recv,
            device_id=device, device_id_type=MESH,
        )

    barrier = pltpu.get_barrier_semaphore()

    def greet_dp(j):
        pl.semaphore_signal(barrier, inc=1, device_id=((d + j) % DP, e), device_id_type=MESH)

    def greet_expert(j):
        pl.semaphore_signal(barrier, inc=1, device_id=(d, (e + j) % EX), device_id_type=MESH)

    loop(1, DP, greet_dp)
    loop(1, EX, greet_expert)

    wt[...] = w_in[...].astype(F32).T.astype(BF16)
    w_all[d] = wt[...]
    own_down = pltpu.make_async_copy(
        ex_down.at[:, :, pl.ds(pl.multiple_of(e * LANE, LANE), LANE)], d_all.at[e], own_sem
    )
    own_down.start()
    named = jnp.zeros((rows, 64), F32)
    experts_iota = iota((rows, 64), 1)
    for k in range(ids.shape[1]):
        named = named + (ids[:, k : k + 1] == experts_iota).astype(F32)
    lower = (iota((rows, rows), 1) < iota((rows, rows), 0)).astype(F32)
    earlier = jnp.dot(lower, named, preferred_element_type=F32)
    slots_iota = iota((rows, DP * RB), 1).astype(F32)
    sel_sum = jnp.zeros((rows, DP * RB), F32)
    comb_sum = jnp.zeros((rows, DP * RB), F32)
    for k in range(ids.shape[1]):
        own = ids[:, k : k + 1]
        place = jnp.sum(jnp.where(own == experts_iota, earlier, 0.0), axis=1, keepdims=True)
        slot = ((own >> 1) * RB + (own & 1) * CAP).astype(F32) + place
        hit = slots_iota == slot
        sel_sum = sel_sum + jnp.where(hit, 1.0, 0.0)
        comb_sum = comb_sum + jnp.where(hit, weights[:, k : k + 1], 0.0)
    sel[...] = sel_sum.astype(BF16)
    comb[...] = comb_sum

    def packed_row(j):
        inner = j & (RB - 1)
        second = (inner >= CAP).astype(jnp.int32)
        row = second * (per_expert - CAP) + (j >> 5) * CAP + inner
        return jnp.where(inner < 2 * CAP, row, -1)

    total = locals_ * per_expert
    pack[...] = (
        packed_row(iota((1, DP * RB), 1)) == iota((total, DP * RB), 0)
    ).astype(F32).astype(BF16)
    unpack[...] = (
        packed_row(iota((DP * RB, 1), 0)) == iota((DP * RB, total), 1)
    ).astype(F32).astype(BF16)

    pl.semaphore_wait(barrier, DP - 1 + EX - 1)

    group = (d // 16) * 4 + (d % 16) // 4
    place4 = d % 4
    run_base = d - place4

    def member(q):
        return (q // 4) * 16 + (q % 4) * 4 + place4

    def send_far(j):
        rcopy(
            wt, w_all.at[d], w_send.at[j], w_recv.at[d], (member((group + j) % 8), e)
        ).start()

    def send_near(src_ref, src, number):
        for i in range(1, 4):
            rcopy(
                src_ref, w_all.at[src], w_send.at[8 + number * 3 + i - 1], w_recv.at[src],
                (run_base + (place4 + i) % 4, e),
            ).start()

    loop(1, 8, send_far)
    send_near(wt, d, 0)

    def down_copy(j):
        other = (e + j) % EX
        return rcopy(
            ex_down.at[:, :, pl.ds(pl.multiple_of(other * LANE, LANE), LANE)], d_all.at[e],
            d_send.at[j], d_recv.at[e], (d, other),
        )

    loop(1, EX, lambda j: down_copy(j).start())

    def relay(j):
        src = member((group - j + 8) % 8)
        rcopy(w_all.at[src], w_all.at[src], w_send.at[0], w_recv.at[src], (src, e)).wait_recv()
        send_near(w_all.at[src], src, j)

    loop(1, 8, relay)

    def near_arrival(j):
        other = run_base + (place4 + 1 + j // 8) % 4
        src = ((j % 8) // 4) * 16 + (j % 4) * 4 + other % 4
        rcopy(w_all.at[src], w_all.at[src], w_send.at[0], w_recv.at[src], (other, e)).wait_recv()

    loop(0, 24, near_arrival)

    head = by_rows(attn[...], w_all[...].reshape(DP * w_all.shape[1], LANE))
    for i in range(EX):
        part[i] = head[:, i * LANE : (i + 1) * LANE]

    def direct(src_of, dst, send, recv, j):
        other = (e + j) % EX
        return rcopy(src_of(other), dst.at[e], send.at[j], recv.at[e], (d, other))

    def direct_arrival(dst, send, recv, j):
        src = (e + EX - j) % EX
        rcopy(dst.at[src], dst.at[src], send.at[0], recv.at[src], (d, src)).wait_recv()

    loop(1, EX, lambda j: direct(lambda o: part.at[o], rs_buf, r_send, r_recv, j).start())
    rs_buf[e] = part[e]
    loop(1, EX, lambda j: direct_arrival(rs_buf, r_send, r_recv, j))
    residual = res_in[...].astype(F32) + jnp.sum(rs_buf[...], axis=0)
    res_all[e] = residual
    loop(1, EX, lambda j: direct(lambda o: res_all.at[e], res_all, g_send, g_recv, j).start())
    loop(1, EX, lambda j: direct_arrival(res_all, g_send, g_recv, j))

    squares = jnp.zeros((rows, LANE), F32)
    for i in range(EX):
        squares = squares + res_all[i] * res_all[i]
    mean = jnp.sum(squares, axis=1, keepdims=True) / (EX * LANE)
    inverse_rms = lax.rsqrt(mean + epsilon)

    normed_own = (residual * inverse_rms * gain[pl.ds(e, 1), :]).astype(BF16)
    xs[...] = by_columns(sel[...], normed_own).astype(BF16).reshape(DP, RB, LANE)

    def over_dp(src, dst, send, recv, j):
        other = (d + j) % DP
        return rcopy(src.at[other], dst.at[d], send.at[j], recv.at[d], (other, e))

    def dp_arrival(dst, send, recv, j):
        src = (d + DP - j) % DP
        rcopy(dst.at[src], dst.at[src], send.at[0], recv.at[src], (src, e)).wait_recv()

    loop(1, DP, lambda j: over_dp(xs, xr, x_send, x_recv, j).start())
    xr[d] = xs[d]

    for i in range(EX):
        normed[:, i * LANE : (i + 1) * LANE] = (
            res_all[i] * inverse_rms * gain[i : i + 1, :]
        ).astype(BF16)
    normed_rows = normed[...]
    shared_active = (
        silu(by_rows(normed_rows, sh_gate[...])) * by_rows(normed_rows, sh_up[...])
    ).astype(BF16)
    shared = jnp.dot(shared_active, sh_down[...], preferred_element_type=F32)
    for i in range(EX):
        s_part[i] = shared[:, i * LANE : (i + 1) * LANE]
    loop(1, EX, lambda j: direct(lambda o: s_part.at[o], s_buf, s_send, s_recv, j).start())
    s_buf[e] = s_part[e]

    loop(1, DP, lambda j: dp_arrival(xr, x_send, x_recv, j))

    chip = e // 2
    core = e % 2
    sibling = e + 1 - 2 * core

    def gather(buf, send, recv):
        def to_chip(j):
            other = ((chip + j) % 8) * 2 + core
            rcopy(buf.at[e], buf.at[e], send.at[j], recv.at[e], (d, other)).start()

        def onward(src, j):
            rcopy(buf.at[src], buf.at[src], send.at[8 + j], recv.at[src], (d, sibling)).start()

        def arrive(j):
            src = ((chip - j + 8) % 8) * 2 + core
            rcopy(buf.at[src], buf.at[src], send.at[0], recv.at[src], (d, src)).wait_recv()
            onward(src, j)

        def from_sibling(j):
            src = ((chip - j + 8) % 8) * 2 + 1 - core
            rcopy(buf.at[src], buf.at[src], send.at[0], recv.at[src], (d, sibling)).wait_recv()

        loop(1, 8, to_chip)
        onward(e, 0)
        loop(1, 8, arrive)
        loop(0, 8, from_sibling)

    def gather_sent(buf, send, recv):
        def sent(j):
            rcopy(buf.at[e], buf.at[e], send.at[j], recv.at[e], (d, sibling)).wait_send()

        loop(1, 16, sent)

    x_all[e] = jnp.dot(
        pack[...], xr[...].reshape(DP * RB, LANE), preferred_element_type=F32
    ).astype(BF16)
    gather(x_all, xa_send, xa_recv)

    for l in range(locals_):
        span = slice(l * per_expert, (l + 1) * per_expert)
        tokens = jnp.concatenate([x_all[i, span, :] for i in range(EX)], axis=1)
        a_all[e, span, :] = (
            silu(by_rows(tokens, ex_gate[l])) * by_rows(tokens, ex_up[l])
        ).astype(BF16)
    gather(a_all, aa_send, aa_recv)

    own_down.wait()
    loop(1, EX, lambda j: direct_arrival(d_all, d_send, d_recv, j))
    results = []
    for l in range(locals_):
        span = slice(l * per_expert, (l + 1) * per_expert)
        y = jnp.zeros((per_expert, LANE), F32)
        for i in range(EX):
            y = y + jnp.dot(a_all[i, span, :], d_all[i, l], preferred_element_type=F32)
        results.append(y.astype(BF16))
    y_rows = jnp.concatenate(results, axis=0)
    ys[...] = (
        jnp.dot(unpack[...], y_rows, preferred_element_type=F32)
        .astype(BF16)
        .reshape(DP, RB, LANE)
    )
    loop(1, DP, lambda j: over_dp(ys, yr, y_send, y_recv, j).start())
    yr[d] = ys[d]

    loop(1, EX, lambda j: direct_arrival(s_buf, s_send, s_recv, j))
    base = res_all[e] + jnp.sum(s_buf[...], axis=0)
    loop(1, DP, lambda j: dp_arrival(yr, y_send, y_recv, j))
    routed = lax.dot_general(
        comb[...], yr[...].reshape(DP * RB, LANE).astype(F32), (((1,), (0,)), ((), ())),
        precision=lax.Precision.HIGHEST, preferred_element_type=F32,
    )
    out[...] = (base + routed).astype(BF16)

    loop(
        1, 32,
        lambda j: rcopy(wt, w_all.at[d], w_send.at[j], w_recv.at[d], (d, sibling)).wait_send(),
    )
    loop(1, EX, lambda j: down_copy(j).wait_send())
    loop(1, EX, lambda j: direct(lambda o: part.at[o], rs_buf, r_send, r_recv, j).wait_send())
    loop(1, EX, lambda j: direct(lambda o: res_all.at[e], res_all, g_send, g_recv, j).wait_send())
    loop(1, EX, lambda j: direct(lambda o: s_part.at[o], s_buf, s_send, s_recv, j).wait_send())
    loop(1, DP, lambda j: over_dp(xs, xr, x_send, x_recv, j).wait_send())
    loop(1, DP, lambda j: over_dp(ys, yr, y_send, y_recv, j).wait_send())
    gather_sent(x_all, xa_send, xa_recv)
    gather_sent(a_all, aa_send, aa_recv)


def shards(
    residual_in, attention_values, out_weight, norm_gain, shared_gate, shared_up, shared_down,
    expert_gate, expert_up, expert_down, expert_ids, gate_weights,
):
    rows = residual_in.shape[0]
    local, hidden, width = expert_gate.shape
    total = local * DP * CAP
    vmem = pl.BlockSpec(memory_space=pltpu.VMEM)

    def sems(n):
        return [pltpu.SemaphoreType.DMA((n,))] * 2

    return pl.pallas_call(
        layer_kernel,
        out_shape=jax.ShapeDtypeStruct((rows, LANE), BF16),
        in_specs=[vmem] * 12,
        out_specs=vmem,
        scratch_shapes=[
            pltpu.VMEM((width // DP, LANE), BF16),
            pltpu.VMEM((DP, width // DP, LANE), BF16),
            pltpu.VMEM((EX, rows, LANE), F32),
            pltpu.VMEM((EX, rows, LANE), F32),
            pltpu.VMEM((EX, rows, LANE), F32),
            pltpu.VMEM((rows, width), BF16),
            pltpu.VMEM((DP, RB, LANE), BF16),
            pltpu.VMEM((DP, RB, LANE), BF16),
            pltpu.VMEM((EX, total, LANE), BF16),
            pltpu.VMEM((EX, total, hidden), BF16),
            pltpu.VMEM((EX, local, hidden, LANE), BF16),
            pltpu.VMEM((EX, rows, LANE), F32),
            pltpu.VMEM((EX, rows, LANE), F32),
            pltpu.VMEM((DP, RB, LANE), BF16),
            pltpu.VMEM((DP, RB, LANE), BF16),
            pltpu.VMEM((total, DP * RB), BF16),
            pltpu.VMEM((DP * RB, total), BF16),
            pltpu.VMEM((rows, DP * RB), BF16),
            pltpu.VMEM((rows, DP * RB), F32),
        ]
        + sems(32) + sems(EX) + sems(EX) + sems(EX) + sems(DP)
        + sems(EX) + sems(EX) + sems(EX) + sems(DP)
        + [pltpu.SemaphoreType.DMA(())],
        compiler_params=pltpu.CompilerParams(
            collective_id=0, has_side_effects=True, vmem_limit_bytes=60 * 1024 * 1024
        ),
        name="layer",
    )(
        residual_in, attention_values, out_weight, norm_gain.reshape(EX, LANE),
        shared_gate, shared_up, shared_down, expert_gate, expert_up, expert_down,
        expert_ids, gate_weights,
    )


def solution(mesh):
    return jax.shard_map(
        shards,
        mesh=mesh,
        in_specs=(
            P("dp", "expert"),
            P("dp", "expert"),
            P("expert", "dp"),
            P(),
            P("expert", None),
            P("expert", None),
            P("expert", None),
            P("dp", "expert", None),
            P("dp", "expert", None),
            P("dp", "expert", None),
            P("dp", None),
            P("dp", None),
        ),
        out_specs=P("dp", "expert"),
        check_vma=False,
    )
```

time: 725 us -> 142 us (0.20)
  waiting for transfers between devices: 426 us -> 0 us
  blocking collectives: 208 us -> 0 us
  Pallas kernels: 0 us -> 137 us
  local copies, waits for them, and re-layouts: 45.1 us -> 4.12 us
  between operations: 13.6 us -> 0.01 us
  matrix products: 12.6 us -> 0 us
  other arithmetic: 9.98 us -> 0 us
    all_to_all x1 -> x0, waiting for transfers between devices: 230 us -> none  [shards(): lax.all_to_all(partials, 'dp', split_axis=0, concat_axis=0, tiled=True)]
    pallas_call x0 -> x1, Pallas kernels: none -> 137 us  [shards(): pl.pallas_call(layer_kernel, out_shape=jax.ShapeDtypeStruct((rows, LANE),...]
    all_to_all x1 -> x0, blocking collectives: 136 us -> none  [shards(): lax.all_to_all(buffer, 'dp', split_axis=0, concat_axis=0, tiled=True)]
    psum x1 -> x0, waiting for transfers between devices: 132 us -> none  [shards(): residual = lax.psum(head_terms, 'expert')]
    all_gather x1 -> x0, blocking collectives: 72.7 us -> none  [shards(): lax.all_gather(out_weight, 'dp', axis=1, tiled=True)]
    reduce_scatter x1 -> x0, waiting for transfers between devices: 64.9 us -> none  [shards(): lax.psum_scatter(shared_terms + routed_terms, 'expert', scatter_dimension...]
    reshape x4 -> x0, local copies, waits for them, and re-layouts: 16.9 us -> none  [the longest x2 7.69 us: shards(): slot_rows.astype(jnp.bfloat16)]
    dot_general x6 -> x0, matrix products: 12.6 us -> none  [the longest x1 5.87 us: expert_apply(): jnp.einsum('slmf,lfd->slmd', active, expert_down, preferred_element_type=...]
  transfers between devices with their start and end apart: 3 -> 0, of which waited for: 3 -> 0; matrix products, arithmetic and copies ran while one was open for 1% -> 0% of each run, Pallas kernels for 0% -> 0%
where the time goes in v1:
time: 142 us; the launch traced here: 141 us
  Pallas kernels  137 us (96%)
  local copies, waits for them, and re-layouts  4.12 us (3%)
    pallas_call x1, Pallas kernels, shards(): pl.pallas_call(layer_kernel, out_shape=jax.ShapeDtypeStruct((rows, LANE),...  137 us
    unnamed x8, local copies, waits for them, and re-layouts  4.12 us

profile of v1, /device:TPU:1, one launch (start us, length us, event | category | flops | bytes accessed | tf_op | source)
XLA Modules:
  0.0 141.5 jit_solution(1673450834238028628)
XLA Ops:
  0.0 0.0 copy-start.1
  0.0 1.4 copy.14.ids
  1.4 0.0 copy-done.1
  1.4 0.0 copy-start
  1.4 0.7 copy.15.weights
  2.1 0.0 copy-done
  2.1 0.7 copy.13.w_in
  2.8 137.4 %layer.1 = bf16[48,128]{1,0:T(8,128)(2,1)} custom-call(bf16[48,128]{1,0:T(8,128)(2,1)} %res_in.1, bf16[48,128]{1,0:T(8,128)(2,1)} %attn.1, bf16[128,64]{1,0:T(8,128)(2,1)} %copy.13.w_in, f32[16,128]{1,0:T(8,128)} %bitcast.1, bf16[176,2048]{1,0:T(8,128)(2,1)} %sh_gate.1, bf16[176,2048]{1,0:T(8,128)(2,1)} %sh_up.1, bf16[176,2048]{1,0:T(8,128)(2,1)} %sh_down.1, ...), custom_call_target="tpu_custom_call" | custom-call | tf_op jit(solution)/shard_map/layer/pallas_call | solution.py:315
  140.2 1.3 copy.17
Async XLA Ops:
  0.0 1.4 copy-start.1
  1.4 0.7 copy-start

commit v2 on v1

v2 whole, which is shorter than its diff:
```python
import jax
import jax.numpy as jnp
from jax import lax
from jax.experimental import pallas as pl
from jax.experimental.pallas import tpu as pltpu
from jax.sharding import PartitionSpec as P

MESH = pl.DeviceIdType.MESH
epsilon = 1e-06
DP = 32
EX = 16
CAP = 10
RB = 16
LANE = 128
F32 = jnp.float32
BF16 = jnp.bfloat16


def by_rows(left, right):
    return lax.dot_general(left, right, (((1,), (1,)), ((), ())), preferred_element_type=F32)


def by_columns(left, right):
    return lax.dot_general(left, right, (((0,), (0,)), ((), ())), preferred_element_type=F32)


def iota(shape, dim):
    return lax.broadcasted_iota(jnp.int32, shape, dim)


def silu(v):
    return v / (1.0 + jnp.exp(-v))


def loop(start, stop, body):
    def step(j, carry):
        body(j)
        return carry

    lax.fori_loop(start, stop, step, 0)


def layer_kernel(
    res_in, attn, w_in, gain, sh_gate_in, sh_up_in, sh_down_in, ex_gate_in, ex_up_in, ex_down,
    ids, weights,
    out,
    sh_gate, sh_up, sh_down, ex_gate, ex_up,
    w_all, part, rs_buf, res_all, xs, xr, x_all, a_all, d_all, s_part, s_buf, ys, yr,
    pack, unpack, sel, comb,
    in_sem, w_send, w_recv, d_send, d_recv, r_send, r_recv, g_send, g_recv, x_send, x_recv,
    xa_send, xa_recv, s_send, s_recv, aa_send, aa_recv, y_send, y_recv,
):
    d = lax.axis_index("dp")
    e = lax.axis_index("expert")
    rows = res_in.shape[0]
    local = ex_gate.shape[0]
    per_expert = DP * CAP
    slots = DP * RB

    def rcopy(src, dst, send, recv, device):
        return pltpu.make_async_remote_copy(
            src_ref=src, dst_ref=dst, send_sem=send, recv_sem=recv,
            device_id=device, device_id_type=MESH,
        )

    def arrival(ref, recv, send, device):
        rcopy(ref, ref, send, recv, device).wait_recv()

    barrier = pltpu.get_barrier_semaphore()

    def greet_dp(j):
        pl.semaphore_signal(barrier, inc=1, device_id=((d + j) % DP, e), device_id_type=MESH)

    def greet_expert(j):
        pl.semaphore_signal(barrier, inc=1, device_id=(d, (e + j) % EX), device_id_type=MESH)

    loop(1, DP, greet_dp)
    loop(1, EX, greet_expert)

    def own_columns(other):
        return ex_down.at[:, :, pl.ds(pl.multiple_of(other * LANE, LANE), LANE)]

    loads = [
        pltpu.make_async_copy(src, dst, in_sem.at[n])
        for n, (src, dst) in enumerate(
            [
                (sh_gate_in, sh_gate), (sh_up_in, sh_up), (sh_down_in, sh_down),
                (ex_gate_in, ex_gate), (ex_up_in, ex_up), (own_columns(e), d_all.at[e]),
            ]
        )
    ]
    for copy in loads:
        copy.start()
    w_all[d] = w_in[...]
    experts_iota = iota((64, rows), 0)
    named = jnp.zeros((64, rows), F32)
    for k in range(ids.shape[0]):
        named = named + (ids[k : k + 1, :] == experts_iota).astype(F32)
    upper = (iota((rows, rows), 0) < iota((rows, rows), 1)).astype(F32)
    earlier = jnp.dot(named, upper, preferred_element_type=F32)
    slots_iota = iota((local * slots, rows), 0).astype(F32)
    sel_sum = jnp.zeros((local * slots, rows), F32)
    comb_sum = jnp.zeros((local * slots, rows), F32)
    for k in range(ids.shape[0]):
        own = ids[k : k + 1, :]
        place = jnp.sum(jnp.where(own == experts_iota, earlier, 0.0), axis=0, keepdims=True)
        slot = ((own & 1) * slots + (own >> 1) * RB).astype(F32) + place
        hit = slots_iota == slot
        sel_sum = sel_sum + jnp.where(hit, 1.0, 0.0)
        comb_sum = comb_sum + jnp.where(hit, weights[k : k + 1, :], 0.0)
    sel[...] = sel_sum.astype(BF16)
    comb[...] = comb_sum

    def packed_row(j):
        inner = j & (RB - 1)
        return jnp.where(inner < CAP, (j >> 4) * CAP + inner, -1)

    pack[...] = (
        packed_row(iota((1, slots), 1)) == iota((per_expert, slots), 0)
    ).astype(F32).astype(BF16)
    unpack[...] = (
        packed_row(iota((slots, 1), 0)) == iota((slots, per_expert), 1)
    ).astype(F32).astype(BF16)

    pl.semaphore_wait(barrier, DP - 1 + EX - 1)

    z = d % 16
    row = d - z
    kind = z % 4
    group = (d // 16) * 4 + z // 4
    above = row + (z + 1) % 16
    below = row + (z + 15) % 16

    def member(q, of):
        return (q // 4) * 16 + (q % 4) * 4 + of

    def w_copy(src, n, device):
        return rcopy(w_all.at[src], w_all.at[src], w_send.at[n], w_recv.at[src], (device, e))

    loop(1, 8, lambda j: rcopy(
        w_in, w_all.at[d], w_send.at[j], w_recv.at[d], (member((group + j) % 8, kind), e)
    ).start())
    for n, device in ((8, above), (9, below)):
        rcopy(w_in, w_all.at[d], w_send.at[n], w_recv.at[d], (device, e)).start()

    def down_copy(j):
        other = (e + j) % EX
        return rcopy(own_columns(other), d_all.at[e], d_send.at[j], d_recv.at[e], (d, other))

    loop(1, EX, lambda j: down_copy(j).start())

    def w_arrival(src, device):
        arrival(w_all.at[src], w_recv.at[src], w_send.at[0], (device, e))

    def far_arrival(j):
        src = member((group + 8 - j) % 8, kind)
        w_arrival(src, src)
        w_copy(src, 8 + 2 * j, above).start()
        w_copy(src, 9 + 2 * j, below).start()

    loop(1, 8, far_arrival)

    def near_low(q):
        src = member(q, (kind + 3) % 4)
        w_arrival(src, below)
        w_copy(src, 24 + q, above).start()
        w_arrival(member(q, (kind + 1) % 4), above)

    def near_high(q):
        src = member(q, (kind + 1) % 4)
        w_arrival(src, above)
        w_copy(src, 24 + q, below).start()
        w_arrival(member(q, (kind + 3) % 4), below)

    loop(0, 4, near_low)
    loop(4, 8, near_high)
    loop(0, 4, lambda q: w_arrival(member(q, (kind + 2) % 4), below))
    loop(4, 8, lambda q: w_arrival(member(q, (kind + 2) % 4), above))

    head = by_rows(attn[...], w_all[...].reshape(DP * w_all.shape[1], LANE))
    for i in range(EX):
        part[i] = head[:, i * LANE : (i + 1) * LANE]

    def direct(src, dst, send, recv, j):
        other = (e + j) % EX
        return rcopy(src.at[other], dst.at[e], send.at[j], recv.at[e], (d, other))

    def direct_arrival(dst, send, recv, j):
        src = (e + EX - j) % EX
        arrival(dst.at[src], recv.at[src], send.at[0], (d, src))

    core = e % 2
    x = (e // 2) % 4
    y = e // 8

    def at(right, other_row):
        yy = y if other_row == 0 else 1 - y
        return (yy * 4 + (x + right) % 4) * 2 + core

    left, right, across = at(3, 0), at(1, 0), at(0, 1)
    sibling = e + 1 - 2 * core

    def gather_start(buf, l, send, recv):
        for n, device in ((1, right), (2, left), (3, across), (4, sibling)):
            rcopy(
                buf.at[l, e], buf.at[l, e], send.at[l, n], recv.at[l, e], (d, device)
            ).start()

    def gather_rest(buf, l, send, recv):
        def take(src, device):
            arrival(buf.at[l, src], recv.at[l, src], send.at[l, 0], (d, device))

        def on(src, n, device):
            rcopy(
                buf.at[l, src], buf.at[l, src], send.at[l, n], recv.at[l, src], (d, device)
            ).start()

        src = left
        take(src, left)
        on(src, 5, right * (1 - core) + across * core)
        on(src, 6, sibling)
        src = across
        take(src, across)

        @pl.when(core == 0)
        def _():
            on(across, 7, right)
            on(across, 8, left)

        on(src, 9, sibling)
        src = right
        take(src, right)

        @pl.when(core == 1)
        def _():
            on(right, 7, left)
            on(right, 8, across)

        on(src, 10, sibling)
        src = at(1, 1)
        take(src, right * (1 - core) + across * core)

        @pl.when(core == 0)
        def _():
            on(at(1, 1), 11, left)

        on(src, 12, sibling)
        src = at(2, 0)
        take(src, left * (1 - core) + right * core)

        @pl.when(core == 1)
        def _():
            on(at(2, 0), 11, across)

        on(src, 13, sibling)
        src = at(3, 1)
        take(src, left * (1 - core) + across * core)
        on(src, 14, sibling)
        src = at(2, 1)
        take(src, right * (1 - core) + across * core)
        on(src, 15, sibling)

        def from_sibling(chip):
            take(chip * 2 + 1 - core, sibling)

        loop(0, 8, from_sibling)

    def gather_sent(buf, l, send, recv):
        loop(
            1, 16,
            lambda n: rcopy(
                buf.at[l, e], buf.at[l, e], send.at[l, n], recv.at[l, e], (d, sibling)
            ).wait_send(),
        )

    loop(1, EX, lambda j: direct(part, rs_buf, r_send, r_recv, j).start())
    rs_buf[e] = part[e]
    loop(1, EX, lambda j: direct_arrival(rs_buf, r_send, r_recv, j))
    residual = res_in[...].astype(F32) + jnp.sum(rs_buf[...], axis=0)
    res_all[0, e] = residual
    gather_start(res_all, 0, g_send, g_recv)
    gather_rest(res_all, 0, g_send, g_recv)

    squares = jnp.zeros((rows, LANE), F32)
    for i in range(EX):
        squares = squares + res_all[0, i] * res_all[0, i]
    mean = jnp.sum(squares, axis=1, keepdims=True) / (EX * LANE)
    inverse_rms = lax.rsqrt(mean + epsilon)

    normed_own = (residual * inverse_rms * gain[pl.ds(e, 1), :]).astype(BF16)

    def over_dp(src, dst, l, send, recv, j):
        other = (d + j) % DP
        return rcopy(src.at[l, other], dst.at[l, d], send.at[l, j], recv.at[l, d], (other, e))

    def dp_arrival(dst, l, send, recv, j):
        src = (d + DP - j) % DP
        arrival(dst.at[l, src], recv.at[l, src], send.at[l, 0], (src, e))

    for l in range(local):
        xs[l] = (
            jnp.dot(
                sel[l * slots : (l + 1) * slots, :], normed_own, preferred_element_type=F32
            ).astype(BF16).reshape(DP, RB, LANE)
        )
        loop(1, DP, lambda j: over_dp(xs, xr, l, x_send, x_recv, j).start())
        xr[l, d] = xs[l, d]

    for copy in loads:
        copy.wait()
    normed = jnp.concatenate(
        [(res_all[0, i] * inverse_rms * gain[i : i + 1, :]).astype(BF16) for i in range(EX)],
        axis=1,
    )
    shared_active = (
        silu(by_rows(normed, sh_gate[...])) * by_rows(normed, sh_up[...])
    ).astype(BF16)
    shared = jnp.dot(shared_active, sh_down[...], preferred_element_type=F32)
    for i in range(EX):
        s_part[i] = shared[:, i * LANE : (i + 1) * LANE]
    s_buf[e] = s_part[e]

    def take_rows(l):
        loop(1, DP, lambda j: dp_arrival(xr, l, x_send, x_recv, j))
        x_all[l, e] = jnp.dot(
            pack[...], xr[l].reshape(slots, LANE), preferred_element_type=F32
        ).astype(BF16)
        gather_start(x_all, l, xa_send, xa_recv)

    def activate(l):
        tokens = jnp.concatenate([x_all[l, i] for i in range(EX)], axis=1)
        a_all[l, e] = (
            silu(by_rows(tokens, ex_gate[l])) * by_rows(tokens, ex_up[l])
        ).astype(BF16)
        gather_start(a_all, l, aa_send, aa_recv)

    def send_back(l):
        y_rows = jnp.zeros((per_expert, LANE), F32)
        for i in range(EX):
            y_rows = y_rows + jnp.dot(a_all[l, i], d_all[i, l], preferred_element_type=F32)
        ys[l] = (
            jnp.dot(unpack[...], y_rows.astype(BF16), preferred_element_type=F32)
            .astype(BF16)
            .reshape(DP, RB, LANE)
        )
        loop(1, DP, lambda j: over_dp(ys, yr, l, y_send, y_recv, j).start())
        yr[l, d] = ys[l, d]

    def collect(l):
        loop(1, DP, lambda j: dp_arrival(yr, l, y_send, y_recv, j))
        return lax.dot_general(
            comb[l * slots : (l + 1) * slots, :], yr[l].reshape(slots, LANE).astype(F32),
            (((0,), (0,)), ((), ())),
            precision=lax.Precision.HIGHEST, preferred_element_type=F32,
        )

    take_rows(0)
    gather_rest(x_all, 0, xa_send, xa_recv)
    take_rows(1)
    activate(0)
    gather_rest(x_all, 1, xa_send, xa_recv)
    activate(1)
    gather_rest(a_all, 0, aa_send, aa_recv)
    loop(1, EX, lambda j: direct_arrival(d_all, d_send, d_recv, j))
    send_back(0)
    gather_rest(a_all, 1, aa_send, aa_recv)
    send_back(1)
    loop(1, EX, lambda j: direct(s_part, s_buf, s_send, s_recv, j).start())
    routed = collect(0)
    loop(1, EX, lambda j: direct_arrival(s_buf, s_send, s_recv, j))
    base = residual + jnp.sum(s_buf[...], axis=0)
    routed = routed + collect(1)
    out[...] = (base + routed).astype(BF16)

    loop(1, 32, lambda n: w_copy(d, n, above).wait_send())
    loop(1, EX, lambda j: down_copy(j).wait_send())
    loop(1, EX, lambda j: direct(part, rs_buf, r_send, r_recv, j).wait_send())
    loop(1, EX, lambda j: direct(s_part, s_buf, s_send, s_recv, j).wait_send())
    gather_sent(res_all, 0, g_send, g_recv)
    for l in range(local):
        loop(1, DP, lambda j: over_dp(xs, xr, l, x_send, x_recv, j).wait_send())
        loop(1, DP, lambda j: over_dp(ys, yr, l, y_send, y_recv, j).wait_send())
        gather_sent(x_all, l, xa_send, xa_recv)
        gather_sent(a_all, l, aa_send, aa_recv)


def shards(
    residual_in, attention_values, out_weight, norm_gain, shared_gate, shared_up, shared_down,
    expert_gate, expert_up, expert_down, expert_ids, gate_weights,
):
    rows = residual_in.shape[0]
    local, hidden, width = expert_gate.shape
    per_expert = DP * CAP
    vmem = pl.BlockSpec(memory_space=pltpu.VMEM)
    hbm = pl.BlockSpec(memory_space=pl.ANY)

    def sems(*shape):
        return [pltpu.SemaphoreType.DMA(shape)] * 2

    def like(array):
        return pltpu.VMEM(array.shape, array.dtype)

    return pl.pallas_call(
        layer_kernel,
        out_shape=jax.ShapeDtypeStruct((rows, LANE), BF16),
        in_specs=[vmem] * 4 + [hbm] * 6 + [vmem] * 2,
        out_specs=vmem,
        scratch_shapes=[
            like(shared_gate), like(shared_up), like(shared_down), like(expert_gate),
            like(expert_up),
            pltpu.VMEM((DP, width // DP, LANE), BF16),
            pltpu.VMEM((EX, rows, LANE), F32),
            pltpu.VMEM((EX, rows, LANE), F32),
            pltpu.VMEM((1, EX, rows, LANE), F32),
            pltpu.VMEM((local, DP, RB, LANE), BF16),
            pltpu.VMEM((local, DP, RB, LANE), BF16),
            pltpu.VMEM((local, EX, per_expert, LANE), BF16),
            pltpu.VMEM((local, EX, per_expert, hidden), BF16),
            pltpu.VMEM((EX, local, hidden, LANE), BF16),
            pltpu.VMEM((EX, rows, LANE), F32),
            pltpu.VMEM((EX, rows, LANE), F32),
            pltpu.VMEM((local, DP, RB, LANE), BF16),
            pltpu.VMEM((local, DP, RB, LANE), BF16),
            pltpu.VMEM((per_expert, DP * RB), BF16),
            pltpu.VMEM((DP * RB, per_expert), BF16),
            pltpu.VMEM((local * DP * RB, rows), BF16),
            pltpu.VMEM((local * DP * RB, rows), F32),
            pltpu.SemaphoreType.DMA((6,)),
        ]
        + sems(DP) + sems(EX) + sems(EX) + sems(1, EX) + sems(local, DP)
        + sems(local, EX) + sems(EX) + sems(local, EX) + sems(local, DP),
        compiler_params=pltpu.CompilerParams(
            collective_id=0, has_side_effects=True, vmem_limit_bytes=60 * 1024 * 1024
        ),
        name="layer",
    )(
        residual_in, attention_values, out_weight.T, norm_gain.reshape(EX, LANE),
        shared_gate, shared_up, shared_down, expert_gate, expert_up, expert_down,
        expert_ids.T, gate_weights.T,
    )


def solution(mesh):
    return jax.shard_map(
        shards,
        mesh=mesh,
        in_specs=(
            P("dp", "expert"),
            P("dp", "expert"),
            P("expert", "dp"),
            P(),
            P("expert", None),
            P("expert", None),
            P("expert", None),
            P("dp", "expert", None),
            P("dp", "expert", None),
            P("dp", "expert", None),
            P("dp", None),
            P("dp", None),
        ),
        out_specs=P("dp", "expert"),
        check_vma=False,
    )
```

time: 142 us -> 135 us (0.951)
  Pallas kernels: 137 us -> 134 us
  local copies, waits for them, and re-layouts: 4.12 us -> 1.31 us
    pallas_call x1, Pallas kernels: 137 us -> 134 us  [shards(): pl.pallas_call(layer_kernel, out_shape=jax.ShapeDtypeStruct((rows, LANE),...]
    unnamed x8 -> x1, local copies, waits for them, and re-layouts: 4.12 us -> 1.31 us
where the time goes in v2:
time: 135 us
  Pallas kernels  134 us (99%)
    pallas_call x1, Pallas kernels, shards(): pl.pallas_call(layer_kernel, out_shape=jax.ShapeDtypeStruct((rows, LANE),...  134 us

profile of v2, /device:TPU:1, one launch (start us, length us, event | category | flops | bytes accessed | tf_op | source)
XLA Modules:
  0.0 134.9 jit_solution(7943065737908266849)
XLA Ops:
  0.0 133.6 %layer.1 = bf16[48,128]{1,0:T(8,128)(2,1)} custom-call(bf16[48,128]{1,0:T(8,128)(2,1)} %res_in.1, bf16[48,128]{1,0:T(8,128)(2,1)} %attn.1, bf16[64,128]{1,0:T(8,128)(2,1)} %bitcast.4, f32[16,128]{1,0:T(8,128)} %bitcast.5, bf16[176,2048]{1,0:T(8,128)(2,1)} %sh_gate_in.1, bf16[176,2048]{1,0:T(8,128)(2,1)} %sh_up_in.1, bf16[176,2048]{1,0:T(8,128)(2,1)} %sh_down_in.1, ...), custom_call_target="tpu_custom_call" | custom-call | tf_op jit(solution)/shard_map/layer/pallas_call | solution.py:403
  133.6 1.3 copy.14

commit v3 on v2

v3 whole, which is shorter than its diff:
```python
import jax
import jax.numpy as jnp
from jax import lax
from jax.experimental import pallas as pl
from jax.experimental.pallas import tpu as pltpu
from jax.sharding import PartitionSpec as P

MESH = pl.DeviceIdType.MESH
epsilon = 1e-06
DP = 32
EX = 16
CAP = 10
RB = 16
LANE = 128
F32 = jnp.float32
BF16 = jnp.bfloat16


def by_rows(left, right):
    return lax.dot_general(left, right, (((1,), (1,)), ((), ())), preferred_element_type=F32)


def by_columns(left, right):
    return lax.dot_general(left, right, (((0,), (0,)), ((), ())), preferred_element_type=F32)


def iota(shape, dim):
    return lax.broadcasted_iota(jnp.int32, shape, dim)


def silu(v):
    return v / (1.0 + jnp.exp(-v))


def loop(start, stop, body):
    def step(j, carry):
        body(j)
        return carry

    lax.fori_loop(start, stop, step, 0)


def layer_kernel(
    res_in, attn, w_in, gain, sh_gate_in, sh_up_in, sh_down_in, ex_gate_in, ex_up_in, ex_down,
    ids, weights,
    out,
    sh_gate, sh_up, sh_down, ex_gate, ex_up,
    w_all, part, rs_buf, res_all, xs, xr, x_own, x_all, a_all, d_all, s_part, s_buf, ys, yr,
    halves, half_in, pack, unpack, sel, comb,
    in_sem, w_send, w_recv, d_send, d_recv, r_send, r_recv, g_send, g_recv, x_send, x_recv,
    xa_send, xa_recv, s_send, s_recv, aa_send, aa_recv, y_send, y_recv, p_send, p_recv,
    h_send, h_recv,
):
    d = lax.axis_index("dp")
    e = lax.axis_index("expert")
    rows = res_in.shape[0]
    hidden = ex_gate.shape[1]
    core = e % 2
    chip = e // 2
    sibling = e + 1 - 2 * core
    z = d % 16
    half = d // 16
    packed = 16 * CAP
    slots = 16 * RB

    def rcopy(src, dst, send, recv, device):
        return pltpu.make_async_remote_copy(
            src_ref=src, dst_ref=dst, send_sem=send, recv_sem=recv,
            device_id=device, device_id_type=MESH,
        )

    def arrival(ref, recv, send, device):
        rcopy(ref, ref, send, recv, device).wait_recv()

    barrier = pltpu.get_barrier_semaphore()

    def greet_dp(j):
        pl.semaphore_signal(barrier, inc=1, device_id=((d + j) % DP, e), device_id_type=MESH)

    def greet_expert(j):
        pl.semaphore_signal(barrier, inc=1, device_id=(d, (e + j) % EX), device_id_type=MESH)

    loop(1, DP, greet_dp)
    loop(1, EX, greet_expert)

    def own_columns(other):
        return ex_down.at[
            other % 2, :, pl.ds(pl.multiple_of((other // 2) * 2 * LANE, 2 * LANE), 2 * LANE)
        ]

    loads = [
        pltpu.make_async_copy(src, dst, in_sem.at[n])
        for n, (src, dst) in enumerate(
            [
                (sh_gate_in, sh_gate), (sh_up_in, sh_up), (sh_down_in, sh_down),
                (ex_gate_in.at[core], ex_gate.at[core]), (ex_up_in.at[core], ex_up.at[core]),
                (own_columns(e), d_all.at[e]),
            ]
        )
    ]
    for copy in loads:
        copy.start()
    w_all[d] = w_in[...]
    experts_iota = iota((64, rows), 0)
    named = jnp.zeros((64, rows), F32)
    for k in range(ids.shape[0]):
        named = named + (ids[k : k + 1, :] == experts_iota).astype(F32)
    upper = (iota((rows, rows), 0) < iota((rows, rows), 1)).astype(F32)
    earlier = jnp.dot(named, upper, preferred_element_type=F32)
    sel_iota = iota((4 * slots, rows), 0).astype(F32)
    comb_iota = iota((2 * slots, rows), 0).astype(F32)
    sel_sum = jnp.zeros((4 * slots, rows), F32)
    comb_sum = jnp.zeros((2 * slots, rows), F32)
    for k in range(ids.shape[0]):
        own = ids[k : k + 1, :]
        place = jnp.sum(jnp.where(own == experts_iota, earlier, 0.0), axis=0, keepdims=True)
        own_z = (own >> 1) & 15
        far = (own >> 5) + half - 2 * (own >> 5) * half
        slot = (far * 2 * slots + own_z * 2 * RB + (own & 1) * RB).astype(F32) + place
        sel_sum = sel_sum + jnp.where(sel_iota == slot, 1.0, 0.0)
        mine = (far * slots + own_z * RB).astype(F32) + place
        mine = jnp.where((own & 1) == core, mine, -1.0)
        comb_sum = comb_sum + jnp.where(comb_iota == mine, weights[k : k + 1, :], 0.0)
    sel[...] = sel_sum.astype(BF16)
    comb[...] = comb_sum

    def packed_row(j):
        inner = j & (RB - 1)
        return jnp.where(inner < CAP, (j >> 4) * CAP + inner, -1)

    pack[...] = (
        packed_row(iota((1, slots), 1)) == iota((packed, slots), 0)
    ).astype(F32).astype(BF16)
    unpack[...] = (
        packed_row(iota((slots, 1), 0)) == iota((slots, packed), 1)
    ).astype(F32).astype(BF16)

    pl.semaphore_wait(barrier, DP - 1 + EX - 1)

    row = d - z
    kind = z % 4
    group = (d // 16) * 4 + z // 4
    above = row + (z + 1) % 16
    below = row + (z + 15) % 16

    def member(q, of):
        return (q // 4) * 16 + (q % 4) * 4 + of

    def w_copy(src, n, device):
        return rcopy(w_all.at[src], w_all.at[src], w_send.at[n], w_recv.at[src], (device, e))

    loop(1, 8, lambda j: rcopy(
        w_in, w_all.at[d], w_send.at[j], w_recv.at[d], (member((group + j) % 8, kind), e)
    ).start())
    for n, device in ((8, above), (9, below)):
        rcopy(w_in, w_all.at[d], w_send.at[n], w_recv.at[d], (device, e)).start()

    def down_copy(j):
        other = (e + j) % EX
        return rcopy(own_columns(other), d_all.at[e], d_send.at[j], d_recv.at[e], (d, other))

    def swap(n, src, dst):
        return rcopy(
            src.at[1 - core], dst.at[core], p_send.at[n], p_recv.at[n], (d, sibling)
        )

    swap(0, ex_gate_in, ex_gate).start()
    swap(1, ex_up_in, ex_up).start()
    loop(1, EX, lambda j: down_copy(j).start())

    def w_arrival(src, device):
        arrival(w_all.at[src], w_recv.at[src], w_send.at[0], (device, e))

    def far_arrival(j):
        src = member((group + 8 - j) % 8, kind)
        w_arrival(src, src)
        w_copy(src, 8 + 2 * j, above).start()
        w_copy(src, 9 + 2 * j, below).start()

    loop(1, 8, far_arrival)

    def near_low(q):
        src = member(q, (kind + 3) % 4)
        w_arrival(src, below)
        w_copy(src, 24 + q, above).start()
        w_arrival(member(q, (kind + 1) % 4), above)

    def near_high(q):
        src = member(q, (kind + 1) % 4)
        w_arrival(src, above)
        w_copy(src, 24 + q, below).start()
        w_arrival(member(q, (kind + 3) % 4), below)

    loop(0, 4, near_low)
    loop(4, 8, near_high)
    loop(0, 4, lambda q: w_arrival(member(q, (kind + 2) % 4), below))
    loop(4, 8, lambda q: w_arrival(member(q, (kind + 2) % 4), above))

    head = by_rows(attn[...], w_all[...].reshape(DP * w_all.shape[1], LANE))
    for i in range(EX):
        part[i] = head[:, i * LANE : (i + 1) * LANE]

    def direct(src, dst, send, recv, j):
        other = (e + j) % EX
        return rcopy(src.at[other], dst.at[e], send.at[j], recv.at[e], (d, other))

    def direct_arrival(dst, send, recv, j):
        src = (e + EX - j) % EX
        arrival(dst.at[src], recv.at[src], send.at[0], (d, src))

    loop(1, EX, lambda j: direct(part, rs_buf, r_send, r_recv, j).start())
    rs_buf[e] = part[e]
    loop(1, EX, lambda j: direct_arrival(rs_buf, r_send, r_recv, j))
    residual = res_in[...].astype(F32) + jnp.sum(rs_buf[...], axis=0)
    res_all[e] = residual

    def res_copy(j):
        other = (e + j) % EX
        return rcopy(res_all.at[e], res_all.at[e], g_send.at[j], g_recv.at[e], (d, other))

    loop(1, EX, lambda j: res_copy(j).start())
    loop(1, EX, lambda j: direct_arrival(res_all, g_send, g_recv, j))

    squares = jnp.zeros((rows, LANE), F32)
    for i in range(EX):
        squares = squares + res_all[i] * res_all[i]
    mean = jnp.sum(squares, axis=1, keepdims=True) / (EX * LANE)
    inverse_rms = lax.rsqrt(mean + epsilon)

    normed_own = (residual * inverse_rms * gain[pl.ds(e, 1), :]).astype(BF16)

    def over_dp(src, dst, h, send, recv, j):
        zz = (z + j) % 16
        other = ((half + h) % 2) * 16 + zz
        return rcopy(src.at[h, zz], dst.at[h, z], send.at[h, j], recv.at[h, z], (other, e))

    def dp_arrivals(dst, h, send, recv):
        def one(j):
            zz = (z + 16 - j) % 16
            other = ((half + h) % 2) * 16 + zz
            arrival(dst.at[h, zz], recv.at[h, zz], send.at[h, 0], (other, e))

        loop(1 - h, 16, one)

    for h in range(2):
        xs[h] = (
            jnp.dot(
                sel[h * 2 * slots : (h + 1) * 2 * slots, :], normed_own,
                preferred_element_type=F32,
            ).astype(BF16).reshape(16, 2, RB, LANE)
        )
        loop(1 - h, 16, lambda j: over_dp(xs, xr, h, x_send, x_recv, j).start())
    xr[0, z] = xs[0, z]

    for copy in loads:
        copy.wait()
    normed = jnp.concatenate(
        [(res_all[i] * inverse_rms * gain[i : i + 1, :]).astype(BF16) for i in range(EX)],
        axis=1,
    )
    shared_active = (
        silu(by_rows(normed, sh_gate[...])) * by_rows(normed, sh_up[...])
    ).astype(BF16)
    shared = jnp.dot(shared_active, sh_down[...], preferred_element_type=F32)
    for i in range(EX):
        s_part[i] = shared[:, i * LANE : (i + 1) * LANE]
    s_buf[e] = s_part[e]

    def x_copy(h, l, j):
        other = ((chip + j) % 8) * 2 + l
        return rcopy(
            x_own.at[h, l], x_all.at[h, e], xa_send.at[h, l * 8 + j], xa_recv.at[h, e],
            (d, other),
        )

    def x_swap(h):
        return rcopy(
            x_own.at[h, 1 - core], x_all.at[h, e], xa_send.at[h, 0], xa_recv.at[h, e],
            (d, sibling),
        )

    def take_rows(h):
        dp_arrivals(xr, h, x_send, x_recv)
        for l in range(2):
            x_own[h, l] = jnp.dot(
                pack[...], xr[h, :, l].reshape(slots, LANE), preferred_element_type=F32
            ).astype(BF16)

        def send(j):
            for l in range(2):
                x_copy(h, l, j).start()

        loop(1, 8, send)
        x_swap(h).start()
        x_all[h, e] = x_own[h, core]

    def a_copy(h, j):
        other = ((chip + j) % 8) * 2 + core
        return rcopy(
            a_all.at[h, chip], a_all.at[h, chip], aa_send.at[h, j], aa_recv.at[h, chip],
            (d, other),
        )

    def activate(h):
        def x_arrival(j):
            src = (e + EX - j) % EX
            arrival(x_all.at[h, src], xa_recv.at[h, src], xa_send.at[h, 0], (d, src))

        loop(1, EX, x_arrival)
        tokens = jnp.concatenate([x_all[h, i] for i in range(EX)], axis=1)
        for b in range(2):
            a_all[h, chip, b] = (
                silu(by_rows(tokens, ex_gate[b])) * by_rows(tokens, ex_up[b])
            ).astype(BF16)
        loop(1, 8, lambda j: a_copy(h, j).start())

    def send_back(h):
        def a_arrival(j):
            src = (chip + 8 - j) % 8
            arrival(
                a_all.at[h, src], aa_recv.at[h, src], aa_send.at[h, 0], (d, src * 2 + core)
            )

        loop(1, 8, a_arrival)
        y_rows = jnp.zeros((packed, 2 * LANE), F32)
        for i in range(EX):
            y_rows = y_rows + jnp.dot(
                a_all[h, i // 2, i % 2], d_all[i], preferred_element_type=F32
            )
        ys[h] = (
            jnp.dot(unpack[...], y_rows.astype(BF16), preferred_element_type=F32)
            .astype(BF16)
            .reshape(16, RB, 2 * LANE)
        )
        loop(1 - h, 16, lambda j: over_dp(ys, yr, h, y_send, y_recv, j).start())

    def collect(h):
        dp_arrivals(yr, h, y_send, y_recv)
        return lax.dot_general(
            comb[h * slots : (h + 1) * slots, :],
            yr[h].reshape(slots, 2 * LANE).astype(F32),
            (((0,), (0,)), ((), ())),
            precision=lax.Precision.HIGHEST, preferred_element_type=F32,
        )

    take_rows(0)
    take_rows(1)
    arrival(ex_gate.at[1 - core], p_recv.at[0], p_send.at[0], (d, sibling))
    arrival(ex_up.at[1 - core], p_recv.at[1], p_send.at[1], (d, sibling))
    activate(0)
    activate(1)
    loop(1, EX, lambda j: direct_arrival(d_all, d_send, d_recv, j))
    send_back(0)
    yr[0, z] = ys[0, z]
    send_back(1)
    loop(1, EX, lambda j: direct(s_part, s_buf, s_send, s_recv, j).start())
    routed = collect(0)
    loop(1, EX, lambda j: direct_arrival(s_buf, s_send, s_recv, j))
    base = residual + jnp.sum(s_buf[...], axis=0)
    routed = routed + collect(1)
    halves[0] = routed[:, :LANE]
    halves[1] = routed[:, LANE:]
    last = rcopy(halves.at[1 - core], half_in, h_send, h_recv, (d, sibling))
    last.start()
    base = base + halves[core]
    last.wait_recv()
    out[...] = (base + half_in[...]).astype(BF16)
    last.wait_send()

    loop(1, 32, lambda n: w_copy(d, n, above).wait_send())
    loop(1, EX, lambda j: down_copy(j).wait_send())
    loop(1, EX, lambda j: direct(part, rs_buf, r_send, r_recv, j).wait_send())
    loop(1, EX, lambda j: direct(s_part, s_buf, s_send, s_recv, j).wait_send())
    loop(1, EX, lambda j: res_copy(j).wait_send())
    swap(0, ex_gate_in, ex_gate).wait_send()
    swap(1, ex_up_in, ex_up).wait_send()
    for h in range(2):
        loop(1 - h, 16, lambda j: over_dp(xs, xr, h, x_send, x_recv, j).wait_send())
        loop(1 - h, 16, lambda j: over_dp(ys, yr, h, y_send, y_recv, j).wait_send())
        loop(1, 8, lambda j: x_copy(h, 0, j).wait_send())
        loop(1, 8, lambda j: x_copy(h, 1, j).wait_send())
        x_swap(h).wait_send()
        loop(1, 8, lambda j: a_copy(h, j).wait_send())


def shards(
    residual_in, attention_values, out_weight, norm_gain, shared_gate, shared_up, shared_down,
    expert_gate, expert_up, expert_down, expert_ids, gate_weights,
):
    rows = residual_in.shape[0]
    local, hidden, width = expert_gate.shape
    packed = 16 * CAP
    vmem = pl.BlockSpec(memory_space=pltpu.VMEM)
    hbm = pl.BlockSpec(memory_space=pl.ANY)

    def sems(*shape):
        return [pltpu.SemaphoreType.DMA(shape)] * 2

    def like(array):
        return pltpu.VMEM(array.shape, array.dtype)

    return pl.pallas_call(
        layer_kernel,
        out_shape=jax.ShapeDtypeStruct((rows, LANE), BF16),
        in_specs=[vmem] * 4 + [hbm] * 6 + [vmem] * 2,
        out_specs=vmem,
        scratch_shapes=[
            like(shared_gate), like(shared_up), like(shared_down), like(expert_gate),
            like(expert_up),
            pltpu.VMEM((DP, width // DP, LANE), BF16),
            pltpu.VMEM((EX, rows, LANE), F32),
            pltpu.VMEM((EX, rows, LANE), F32),
            pltpu.VMEM((EX, rows, LANE), F32),
            pltpu.VMEM((2, 16, 2, RB, LANE), BF16),
            pltpu.VMEM((2, 16, 2, RB, LANE), BF16),
            pltpu.VMEM((2, 2, packed, LANE), BF16),
            pltpu.VMEM((2, EX, packed, LANE), BF16),
            pltpu.VMEM((2, 8, 2, packed, hidden), BF16),
            pltpu.VMEM((EX, hidden, 2 * LANE), BF16),
            pltpu.VMEM((EX, rows, LANE), F32),
            pltpu.VMEM((EX, rows, LANE), F32),
            pltpu.VMEM((2, 16, RB, 2 * LANE), BF16),
            pltpu.VMEM((2, 16, RB, 2 * LANE), BF16),
            pltpu.VMEM((2, rows, LANE), F32),
            pltpu.VMEM((rows, LANE), F32),
            pltpu.VMEM((packed, 16 * RB), BF16),
            pltpu.VMEM((16 * RB, packed), BF16),
            pltpu.VMEM((64 * RB, rows), BF16),
            pltpu.VMEM((32 * RB, rows), F32),
            pltpu.SemaphoreType.DMA((6,)),
        ]
        + sems(DP) + sems(EX) + sems(EX) + sems(EX) + sems(2, 16)
        + sems(2, EX) + sems(EX) + sems(2, 8) + sems(2, 16) + sems(2) + sems(),
        compiler_params=pltpu.CompilerParams(
            collective_id=0, has_side_effects=True, vmem_limit_bytes=60 * 1024 * 1024
        ),
        name="layer",
    )(
        residual_in, attention_values, out_weight.T, norm_gain.reshape(EX, LANE),
        shared_gate, shared_up, shared_down, expert_gate, expert_up, expert_down,
        expert_ids.T, gate_weights.T,
    )


def solution(mesh):
    return jax.shard_map(
        shards,
        mesh=mesh,
        in_specs=(
            P("dp", "expert"),
            P("dp", "expert"),
            P("expert", "dp"),
            P(),
            P("expert", None),
            P("expert", None),
            P("expert", None),
            P("dp", "expert", None),
            P("dp", "expert", None),
            P("dp", "expert", None),
            P("dp", None),
            P("dp", None),
        ),
        out_specs=P("dp", "expert"),
        check_vma=False,
    )
```

time: 135 us -> 117 us (0.87)
  Pallas kernels: 134 us -> 115 us
    pallas_call x1, Pallas kernels: 134 us -> 115 us  [shards(): pl.pallas_call(layer_kernel, out_shape=jax.ShapeDtypeStruct((rows, LANE),...]
where the time goes in v3:
time: 117 us; the launch traced here: 116 us
  Pallas kernels  115 us (98%)
  local copies, waits for them, and re-layouts  1.31 us (1%)
    pallas_call x1, Pallas kernels, shards(): pl.pallas_call(layer_kernel, out_shape=jax.ShapeDtypeStruct((rows, LANE),...  115 us

profile of v3, /device:TPU:1, one launch (start us, length us, event | category | flops | bytes accessed | tf_op | source)
XLA Modules:
  0.0 116.3 jit_solution(8306030408214868764)
XLA Ops:
  0.0 115.0 %layer.1 = bf16[48,128]{1,0:T(8,128)(2,1)} custom-call(bf16[48,128]{1,0:T(8,128)(2,1)} %res_in.1, bf16[48,128]{1,0:T(8,128)(2,1)} %attn.1, bf16[64,128]{1,0:T(8,128)(2,1)} %bitcast.4, f32[16,128]{1,0:T(8,128)} %bitcast.5, bf16[176,2048]{1,0:T(8,128)(2,1)} %sh_gate_in.1, bf16[176,2048]{1,0:T(8,128)(2,1)} %sh_up_in.1, bf16[176,2048]{1,0:T(8,128)(2,1)} %sh_down_in.1, ...), custom_call_target="tpu_custom_call" | custom-call | tf_op jit(solution)/shard_map/layer/pallas_call | solution.py:402
  115.0 1.3 %copy.14 = bf16[48,128]{1,0:T(8,128)(2,1)} copy(bf16[48,128]{1,0:T(8,128)(2,1)} %layer.1) | data formatting | bytes 24576

commit v4 on v3

--- a/solution.py
+++ b/solution.py
@@ -45,9 +45,9 @@
     ids, weights,
     out,
     sh_gate, sh_up, sh_down, ex_gate, ex_up,
-    w_all, part, rs_buf, res_all, xs, xr, x_own, x_all, a_all, d_all, s_part, s_buf, ys, yr,
+    w_all, part, rs_buf, sq_all, n_all, xs, xr, x_own, x_all, a_all, d_all, s_part, s_buf, ys, yr,
     halves, half_in, pack, unpack, sel, comb,
-    in_sem, w_send, w_recv, d_send, d_recv, r_send, r_recv, g_send, g_recv, x_send, x_recv,
+    in_sem, w_send, w_recv, d_send, d_recv, r_send, r_recv, q_send, q_recv, g_send, g_recv, x_send, x_recv,
     xa_send, xa_recv, s_send, s_recv, aa_send, aa_recv, y_send, y_recv, p_send, p_recv,
     h_send, h_recv,
 ):
@@ -164,10 +164,6 @@
             src.at[1 - core], dst.at[core], p_send.at[n], p_recv.at[n], (d, sibling)
         )
 
-    swap(0, ex_gate_in, ex_gate).start()
-    swap(1, ex_up_in, ex_up).start()
-    loop(1, EX, lambda j: down_copy(j).start())
-
     def w_arrival(src, device):
         arrival(w_all.at[src], w_recv.at[src], w_send.at[0], (device, e))
 
@@ -178,6 +174,9 @@
         w_copy(src, 9 + 2 * j, below).start()
 
     loop(1, 8, far_arrival)
+    loop(1, EX, lambda j: down_copy(j).start())
+    swap(0, ex_gate_in, ex_gate).start()
+    swap(1, ex_up_in, ex_up).start()
 
     def near_low(q):
         src = member(q, (kind + 3) % 4)
@@ -212,22 +211,25 @@
     rs_buf[e] = part[e]
     loop(1, EX, lambda j: direct_arrival(rs_buf, r_send, r_recv, j))
     residual = res_in[...].astype(F32) + jnp.sum(rs_buf[...], axis=0)
-    res_all[e] = residual
-
-    def res_copy(j):
+    def to_all(buf, send, recv, j):
         other = (e + j) % EX
-        return rcopy(res_all.at[e], res_all.at[e], g_send.at[j], g_recv.at[e], (d, other))
-
-    loop(1, EX, lambda j: res_copy(j).start())
-    loop(1, EX, lambda j: direct_arrival(res_all, g_send, g_recv, j))
-
-    squares = jnp.zeros((rows, LANE), F32)
-    for i in range(EX):
-        squares = squares + res_all[i] * res_all[i]
-    mean = jnp.sum(squares, axis=1, keepdims=True) / (EX * LANE)
+        return rcopy(buf.at[e], buf.at[e], send.at[j], recv.at[e], (d, other))
+
+    def exact(left, right, contract):
+        return lax.dot_general(
+            left, right, (contract, ((), ())),
+            precision=lax.Precision.HIGHEST, preferred_element_type=F32,
+        )
+
+    sq_all[e] = exact(jnp.ones((8, LANE), F32), residual * residual, ((1,), (1,)))
+    loop(1, EX, lambda j: to_all(sq_all, q_send, q_recv, j).start())
+    loop(1, EX, lambda j: direct_arrival(sq_all, q_send, q_recv, j))
+    squares = jnp.sum(sq_all[...], axis=0)
+    mean = exact(squares, jnp.full((8, LANE), 0.125 / (EX * LANE), F32), ((0,), (0,)))
     inverse_rms = lax.rsqrt(mean + epsilon)
 
     normed_own = (residual * inverse_rms * gain[pl.ds(e, 1), :]).astype(BF16)
+    n_all[e] = normed_own
 
     def over_dp(src, dst, h, send, recv, j):
         zz = (z + j) % 16
@@ -251,13 +253,12 @@
         )
         loop(1 - h, 16, lambda j: over_dp(xs, xr, h, x_send, x_recv, j).start())
     xr[0, z] = xs[0, z]
+    loop(1, EX, lambda j: to_all(n_all, g_send, g_recv, j).start())
 
     for copy in loads:
         copy.wait()
-    normed = jnp.concatenate(
-        [(res_all[i] * inverse_rms * gain[i : i + 1, :]).astype(BF16) for i in range(EX)],
-        axis=1,
-    )
+    loop(1, EX, lambda j: direct_arrival(n_all, g_send, g_recv, j))
+    normed = jnp.concatenate([n_all[i] for i in range(EX)], axis=1)
     shared_active = (
         silu(by_rows(normed, sh_gate[...])) * by_rows(normed, sh_up[...])
     ).astype(BF16)
@@ -371,7 +372,8 @@
     loop(1, EX, lambda j: down_copy(j).wait_send())
     loop(1, EX, lambda j: direct(part, rs_buf, r_send, r_recv, j).wait_send())
     loop(1, EX, lambda j: direct(s_part, s_buf, s_send, s_recv, j).wait_send())
-    loop(1, EX, lambda j: res_copy(j).wait_send())
+    loop(1, EX, lambda j: to_all(sq_all, q_send, q_recv, j).wait_send())
+    loop(1, EX, lambda j: to_all(n_all, g_send, g_recv, j).wait_send())
     swap(0, ex_gate_in, ex_gate).wait_send()
     swap(1, ex_up_in, ex_up).wait_send()
     for h in range(2):
@@ -410,7 +412,8 @@
             pltpu.VMEM((DP, width // DP, LANE), BF16),
             pltpu.VMEM((EX, rows, LANE), F32),
             pltpu.VMEM((EX, rows, LANE), F32),
-            pltpu.VMEM((EX, rows, LANE), F32),
+            pltpu.VMEM((EX, 8, rows), F32),
+            pltpu.VMEM((EX, rows, LANE), BF16),
             pltpu.VMEM((2, 16, 2, RB, LANE), BF16),
             pltpu.VMEM((2, 16, 2, RB, LANE), BF16),
             pltpu.VMEM((2, 2, packed, LANE), BF16),
@@ -429,7 +432,7 @@
             pltpu.VMEM((32 * RB, rows), F32),
             pltpu.SemaphoreType.DMA((6,)),
         ]
-        + sems(DP) + sems(EX) + sems(EX) + sems(EX) + sems(2, 16)
+        + sems(DP) + sems(EX) + sems(EX) + sems(EX) + sems(EX) + sems(2, 16)
         + sems(2, EX) + sems(EX) + sems(2, 8) + sems(2, 16) + sems(2) + sems(),
         compiler_params=pltpu.CompilerParams(
             collective_id=0, has_side_effects=True, vmem_limit_bytes=60 * 1024 * 1024

time: 117 us -> 115 us (0.983)
  Pallas kernels: 115 us -> 113 us
    pallas_call x1, Pallas kernels: 115 us -> 113 us  [shards(): pl.pallas_call(layer_kernel, out_shape=jax.ShapeDtypeStruct((rows, LANE),...]
where the time goes in v4:
time: 115 us; the launch traced here: 114 us
  Pallas kernels  113 us (98%)
  local copies, waits for them, and re-layouts  1.31 us (1%)
    pallas_call x1, Pallas kernels, shards(): pl.pallas_call(layer_kernel, out_shape=jax.ShapeDtypeStruct((rows, LANE),...  113 us

profile of v4, /device:TPU:1, one launch (start us, length us, event | category | flops | bytes accessed | tf_op | source)
XLA Modules:
  0.0 114.3 jit_solution(7803869499468517732)
XLA Ops:
  0.0 113.0 %layer.1 = bf16[48,128]{1,0:T(8,128)(2,1)} custom-call(bf16[48,128]{1,0:T(8,128)(2,1)} %res_in.1, bf16[48,128]{1,0:T(8,128)(2,1)} %attn.1, bf16[64,128]{1,0:T(8,128)(2,1)} %bitcast.4, f32[16,128]{1,0:T(8,128)} %bitcast.5, bf16[176,2048]{1,0:T(8,128)(2,1)} %sh_gate_in.1, bf16[176,2048]{1,0:T(8,128)(2,1)} %sh_up_in.1, bf16[176,2048]{1,0:T(8,128)(2,1)} %sh_down_in.1, ...), custom_call_target="tpu_custom_call" | custom-call | tf_op jit(solution)/shard_map/layer/pallas_call | solution.py:404
  113.0 1.3 %copy.14 = bf16[48,128]{1,0:T(8,128)(2,1)} copy(bf16[48,128]{1,0:T(8,128)(2,1)} %layer.1) | data formatting | bytes 24576

commit v5 on v4

--- a/solution.py
+++ b/solution.py
@@ -231,6 +231,9 @@
     normed_own = (residual * inverse_rms * gain[pl.ds(e, 1), :]).astype(BF16)
     n_all[e] = normed_own
 
+    def far_first(t):
+        return (8 + (t // 2) * (1 - 2 * (t % 2))) % 16
+
     def over_dp(src, dst, h, send, recv, j):
         zz = (z + j) % 16
         other = ((half + h) % 2) * 16 + zz
@@ -251,9 +254,89 @@
                 preferred_element_type=F32,
             ).astype(BF16).reshape(16, 2, RB, LANE)
         )
-        loop(1 - h, 16, lambda j: over_dp(xs, xr, h, x_send, x_recv, j).start())
+        loop(1, 16 + h, lambda t: over_dp(xs, xr, h, x_send, x_recv, far_first(t)).start())
     xr[0, z] = xs[0, z]
     loop(1, EX, lambda j: to_all(n_all, g_send, g_recv, j).start())
+
+    def x_copy(h, l, j):
+        other = ((chip + j) % 8) * 2 + l
+        return rcopy(
+            x_own.at[h, l], x_all.at[h, e], xa_send.at[h, l * 8 + j], xa_recv.at[h, e],
+            (d, other),
+        )
+
+    def x_swap(h):
+        return rcopy(
+            x_own.at[h, 1 - core], x_all.at[h, e], xa_send.at[h, 0], xa_recv.at[h, e],
+            (d, sibling),
+        )
+
+    def take_rows(h):
+        dp_arrivals(xr, h, x_send, x_recv)
+        for l in range(2):
+            x_own[h, l] = jnp.dot(
+                pack[...], xr[h, :, l].reshape(slots, LANE), preferred_element_type=F32
+            ).astype(BF16)
+
+        def send(j):
+            for l in range(2):
+                x_copy(h, l, j).start()
+
+        loop(1, 8, send)
+        x_swap(h).start()
+        x_all[h, e] = x_own[h, core]
+
+    def a_copy(h, j):
+        other = ((chip + j) % 8) * 2 + core
+        return rcopy(
+            a_all.at[h, chip], a_all.at[h, chip], aa_send.at[h, j], aa_recv.at[h, chip],
+            (d, other),
+        )
+
+    def activate(h):
+        def x_arrival(j):
+            src = (e + EX - j) % EX
+            arrival(x_all.at[h, src], xa_recv.at[h, src], xa_send.at[h, 0], (d, src))
+
+        loop(1, EX, x_arrival)
+        tokens = jnp.concatenate([x_all[h, i] for i in range(EX)], axis=1)
+        for b in range(2):
+            a_all[h, chip, b] = (
+                silu(by_rows(tokens, ex_gate[b])) * by_rows(tokens, ex_up[b])
+            ).astype(BF16)
+        loop(1, 8, lambda j: a_copy(h, j).start())
+
+    def send_back(h):
+        def a_arrival(j):
+            src = (chip + 8 - j) % 8
+            arrival(
+                a_all.at[h, src], aa_recv.at[h, src], aa_send.at[h, 0], (d, src * 2 + core)
+            )
+
+        loop(1, 8, a_arrival)
+        y_rows = jnp.zeros((packed, 2 * LANE), F32)
+        for i in range(EX):
+            y_rows = y_rows + jnp.dot(
+                a_all[h, i // 2, i % 2], d_all[i], preferred_element_type=F32
+            )
+        ys[h] = (
+            jnp.dot(unpack[...], y_rows.astype(BF16), preferred_element_type=F32)
+            .astype(BF16)
+            .reshape(16, RB, 2 * LANE)
+        )
+        loop(1, 16 + h, lambda t: over_dp(ys, yr, h, y_send, y_recv, far_first(t)).start())
+
+    def collect(h):
+        dp_arrivals(yr, h, y_send, y_recv)
+        return lax.dot_general(
+            comb[h * slots : (h + 1) * slots, :],
+            yr[h].reshape(slots, 2 * LANE).astype(F32),
+            (((0,), (0,)), ((), ())),
+            precision=lax.Precision.HIGHEST, preferred_element_type=F32,
+        )
+
+    take_rows(0)
+    take_rows(1)
 
     for copy in loads:
         copy.wait()
@@ -267,85 +350,6 @@
         s_part[i] = shared[:, i * LANE : (i + 1) * LANE]
     s_buf[e] = s_part[e]
 
-    def x_copy(h, l, j):
-        other = ((chip + j) % 8) * 2 + l
-        return rcopy(
-            x_own.at[h, l], x_all.at[h, e], xa_send.at[h, l * 8 + j], xa_recv.at[h, e],
-            (d, other),
-        )
-
-    def x_swap(h):
-        return rcopy(
-            x_own.at[h, 1 - core], x_all.at[h, e], xa_send.at[h, 0], xa_recv.at[h, e],
-            (d, sibling),
-        )
-
-    def take_rows(h):
-        dp_arrivals(xr, h, x_send, x_recv)
-        for l in range(2):
-            x_own[h, l] = jnp.dot(
-                pack[...], xr[h, :, l].reshape(slots, LANE), preferred_element_type=F32
-            ).astype(BF16)
-
-        def send(j):
-            for l in range(2):
-                x_copy(h, l, j).start()
-
-        loop(1, 8, send)
-        x_swap(h).start()
-        x_all[h, e] = x_own[h, core]
-
-    def a_copy(h, j):
-        other = ((chip + j) % 8) * 2 + core
-        return rcopy(
-            a_all.at[h, chip], a_all.at[h, chip], aa_send.at[h, j], aa_recv.at[h, chip],
-            (d, other),
-        )
-
-    def activate(h):
-        def x_arrival(j):
-            src = (e + EX - j) % EX
-            arrival(x_all.at[h, src], xa_recv.at[h, src], xa_send.at[h, 0], (d, src))
-
-        loop(1, EX, x_arrival)
-        tokens = jnp.concatenate([x_all[h, i] for i in range(EX)], axis=1)
-        for b in range(2):
-            a_all[h, chip, b] = (
-                silu(by_rows(tokens, ex_gate[b])) * by_rows(tokens, ex_up[b])
-            ).astype(BF16)
-        loop(1, 8, lambda j: a_copy(h, j).start())
-
-    def send_back(h):
-        def a_arrival(j):
-            src = (chip + 8 - j) % 8
-            arrival(
-                a_all.at[h, src], aa_recv.at[h, src], aa_send.at[h, 0], (d, src * 2 + core)
-            )
-
-        loop(1, 8, a_arrival)
-        y_rows = jnp.zeros((packed, 2 * LANE), F32)
-        for i in range(EX):
-            y_rows = y_rows + jnp.dot(
-                a_all[h, i // 2, i % 2], d_all[i], preferred_element_type=F32
-            )
-        ys[h] = (
-            jnp.dot(unpack[...], y_rows.astype(BF16), preferred_element_type=F32)
-            .astype(BF16)
-            .reshape(16, RB, 2 * LANE)
-        )
-        loop(1 - h, 16, lambda j: over_dp(ys, yr, h, y_send, y_recv, j).start())
-
-    def collect(h):
-        dp_arrivals(yr, h, y_send, y_recv)
-        return lax.dot_general(
-            comb[h * slots : (h + 1) * slots, :],
-            yr[h].reshape(slots, 2 * LANE).astype(F32),
-            (((0,), (0,)), ((), ())),
-            precision=lax.Precision.HIGHEST, preferred_element_type=F32,
-        )
-
-    take_rows(0)
-    take_rows(1)
     arrival(ex_gate.at[1 - core], p_recv.at[0], p_send.at[0], (d, sibling))
     arrival(ex_up.at[1 - core], p_recv.at[1], p_send.at[1], (d, sibling))
     activate(0)

time: 115 us -> 114 us (level)
  no operation moved by 1% of the time
where the time goes in v5:
time: 114 us
  Pallas kernels  113 us (99%)
  local copies, waits for them, and re-layouts  1.31 us (1%)
    pallas_call x1, Pallas kernels, shards(): pl.pallas_call(layer_kernel, out_shape=jax.ShapeDtypeStruct((rows, LANE),...  113 us

profile of v5, /device:TPU:1, one launch (start us, length us, event | category | flops | bytes accessed | tf_op | source)
XLA Modules:
  0.0 114.0 jit_solution(12881014419913148537)
XLA Ops:
  0.0 112.7 %layer.1 = bf16[48,128]{1,0:T(8,128)(2,1)} custom-call(bf16[48,128]{1,0:T(8,128)(2,1)} %res_in.1, bf16[48,128]{1,0:T(8,128)(2,1)} %attn.1, bf16[64,128]{1,0:T(8,128)(2,1)} %bitcast.4, f32[16,128]{1,0:T(8,128)} %bitcast.5, bf16[176,2048]{1,0:T(8,128)(2,1)} %sh_gate_in.1, bf16[176,2048]{1,0:T(8,128)(2,1)} %sh_up_in.1, bf16[176,2048]{1,0:T(8,128)(2,1)} %sh_down_in.1, ...), custom_call_target="tpu_custom_call" | custom-call | tf_op jit(solution)/shard_map/layer/pallas_call | solution.py:408
  112.7 1.3 %copy.14 = bf16[48,128]{1,0:T(8,128)(2,1)} copy(bf16[48,128]{1,0:T(8,128)(2,1)} %layer.1) | data formatting | bytes 24576
